TPU v7x, 32 devices: a whole 2x2x4 slice. The times are simulated.
32 devices in a mesh: lon: 4 (over y, core), lat: 8 (over z, x).
Axes of the slice: x: 2, y: 2, z: 4, core: 2. Of those that a mesh axis runs over, the one named last changes fastest.
Arguments:
- eta_adj: float32 [2048, 2048], P('lat', 'lon'), may hold values from -6 to 6
- east_adj: float32 [2048, 2048], P('lat', 'lon'), may hold values from -6 to 6
- north_adj: float32 [2048, 2048], P('lat', 'lon'), may hold values from -6 to 6
- depth: float32 [2048, 2048], P('lat', 'lon'), may hold values from 0.5 to 3
- station_owner: int32 [32768, 1], P(('lon', 'lat')), may hold values from 0 to 31; in each aligned block of 1024 rows (0 to 1023, 1024 to 2047, ...) at most 64 rows name the same one
- station_cell: int32 [32768], P(('lon', 'lat')), may hold values from 0 to 131071
- station_misfit: float32 [32768], P(('lon', 'lat')), may hold values from -6 to 6
- footprints: float32 [8192, 1024], P(('lon', 'lat')), may hold values from -0.1875 to 0.1875
- foot_tile: int32 [8192, 1], P(('lon', 'lat')), may hold values from 0 to 31; in each aligned block of 256 rows (0 to 255, 256 to 511, ...) at most 16 rows name the same one
- foot_block: int32 [8192], P(('lon', 'lat')), may hold values from 0 to 127
- foot_source: int32 [8192], P(('lon', 'lat')), may hold values from 0 to 19
Outputs:
- eta_start: float32 [2048, 2048], P('lat', 'lon')
- east_start: float32 [2048, 2048], P('lat', 'lon')
- north_start: float32 [2048, 2048], P('lat', 'lon')
- uplift_grad: float32 [4, 640], P(None, ('lon', 'lat'))
Inputs may be any that keep to these rules, and one draw needn't show every extreme that they name: `station_owner`: in each device's 1024 rows (aligned blocks), no tile is named by more than 64 rows; some tile is named by exactly 64. `foot_tile`: in each device's 256 rows (aligned blocks), no tile is named by more than 16 rows; some tile is named by exactly 16.
All inputs are finite; a program needn't handle non-finite values.
Results may differ from a plain program's by a relative error of at most 0.0003.
Values sent between devices are 32-bit elements; how exact they have to be, the bound alone decides.
A program may use at most 64 MiB of HBM per device.

v0:
```python
import jax
import jax.numpy as jnp
from jax import lax
from jax.sharding import PartitionSpec as P

ITERS = 4
STA_DEV = 256
SRC_DEV = 20
BH = 8
BW = 128


GRAVITY_STEP = 0.8
DEPTH_STEP = 0.8
TURN_RATE = 0.1
RETAIN = 0.97


def padded_2(array, sides, width):
    for axis, dim in sides:
        size, length = (lax.axis_size(axis), array.shape[dim])
        up = [(i, (i + 1) % size) for i in range(size - 1)]
        down = [(j, i) for i, j in up]
        last = lax.slice_in_dim(array, length - width, length, axis=dim)
        first = lax.slice_in_dim(array, 0, width, axis=dim)
        before = lax.ppermute(last, axis, up)
        after = lax.ppermute(first, axis, down)
        array = jnp.concatenate([before, array, after], axis=dim)
    return array


def east_diff(padded):
    return 0.5 * (padded[..., 1:-1, 2:] - padded[..., 1:-1, :-2])


def north_diff(padded):
    return 0.5 * (padded[..., 2:, 1:-1] - padded[..., :-2, 1:-1])


def slot_positions(target, devices, limit):
    one_hot = (target[:, None] == jnp.arange(devices, dtype=jnp.int32)[None, :]).astype(jnp.int32)
    running = jnp.cumsum(one_hot, axis=0)
    ranking = jnp.sum(running * one_hot, axis=1) - 1
    return target * limit + ranking


def tile_blocks(height):
    rows_here, cols_here = height.shape
    shaped = height.reshape(rows_here // BH, BH, cols_here // BW, BW)
    return shaped.transpose(0, 2, 1, 3).reshape(-1, BH * BW)


def shards(
    eta_adj,
    east_adj,
    north_adj,
    depth,
    station_owner,
    station_cell,
    station_misfit,
    footprints,
    foot_tile,
    foot_block,
    foot_source,
):
    lon_count = lax.axis_size("lon")
    lat_count = lax.axis_size("lat")
    devices = lon_count * lat_count
    rows_here, cols_here = eta_adj.shape
    cells = rows_here * cols_here
    records = station_cell.shape[0]
    capacity = max(2, 2 * records // devices)
    station_place = slot_positions(station_owner[:, 0], devices, capacity)
    period_of = jnp.arange(records, dtype=jnp.int32) // STA_DEV
    coded_cell = (period_of * cells + station_cell).astype(jnp.float32)
    packet = jnp.zeros((2, devices * capacity), jnp.float32)
    packet = packet.at[0, station_place].set(station_misfit).at[1, station_place].set(coded_cell)
    packet = packet.reshape(2, lon_count, lat_count, capacity)
    arrived = lax.all_to_all(
        lax.all_to_all(packet, "lon", split_axis=1, concat_axis=1, tiled=True),
        "lat",
        split_axis=2,
        concat_axis=2,
        tiled=True,
    )
    landing = arrived[1].reshape(-1).astype(jnp.int32)
    amounts = arrived[0].reshape(-1)
    forcing = jnp.zeros((ITERS * cells,), jnp.float32).at[landing].add(amounts)
    forcing = forcing.reshape(ITERS, rows_here, cols_here)
    feet = footprints.shape[0]
    foot_limit = max(2, 2 * feet // devices)
    foot_place = slot_positions(foot_tile[:, 0], devices, foot_limit)
    wanted_ids = (
        jnp.zeros((devices * foot_limit,), jnp.float32)
        .at[foot_place]
        .set(foot_block.astype(jnp.float32))
    )
    wanted_ids = wanted_ids.reshape(lon_count, lat_count, foot_limit)
    foot_buffer = (
        jnp.zeros((devices * foot_limit, BH * BW), jnp.float32).at[foot_place].set(footprints)
    )
    foot_buffer = foot_buffer.reshape(lon_count, lat_count, foot_limit, BH * BW)
    held_feet, held_ids = (
        lax.all_to_all(
            lax.all_to_all(foot_buffer, "lon", split_axis=0, concat_axis=0, tiled=True),
            "lat",
            split_axis=1,
            concat_axis=1,
            tiled=True,
        ),
        lax.all_to_all(
            lax.all_to_all(wanted_ids, "lon", split_axis=0, concat_axis=0, tiled=True),
            "lat",
            split_axis=1,
            concat_axis=1,
            tiled=True,
        ),
    )
    held_index = held_ids.astype(jnp.int32)
    measures = [None] * ITERS
    height, east, north = (eta_adj, east_adj, north_adj)
    for period in range(ITERS - 1, -1, -1):
        flows = padded_2(jnp.stack([east, north]), (("lon", 2), ("lat", 1)), 1)
        pressure = (
            height + forcing[period] - GRAVITY_STEP * (east_diff(flows[0]) + north_diff(flows[1]))
        )
        flux = padded_2(depth * pressure, (("lon", 1), ("lat", 0)), 1)
        east_new = RETAIN * east + TURN_RATE * north - DEPTH_STEP * east_diff(flux)
        north_new = RETAIN * north - TURN_RATE * east - DEPTH_STEP * north_diff(flux)
        height, east, north = (pressure, east_new, north_new)
        measures[period] = jnp.sum(tile_blocks(height)[held_index] * held_feet, axis=-1)
    collected = jnp.stack(measures, axis=-1)
    collected = lax.all_to_all(
        lax.all_to_all(collected, "lon", split_axis=0, concat_axis=0, tiled=True),
        "lat",
        split_axis=1,
        concat_axis=1,
        tiled=True,
    )
    by_row = collected.reshape(devices * foot_limit, ITERS)[foot_place]
    source_hot = (foot_source[:, None] == jnp.arange(SRC_DEV, dtype=jnp.int32)[None, :]).astype(
        jnp.float32
    )
    uplift_grad = jnp.dot(by_row.T, source_hot, precision=lax.Precision.HIGHEST)
    return (height, east, north, uplift_grad)


def solution(mesh):
    in_specs = (
        P("lat", "lon"),
        P("lat", "lon"),
        P("lat", "lon"),
        P("lat", "lon"),
        P(("lon", "lat"), None),
        P(("lon", "lat")),
        P(("lon", "lat")),
        P(("lon", "lat"), None),
        P(("lon", "lat"), None),
        P(("lon", "lat")),
        P(("lon", "lat")),
    )
    out_specs = (P("lat", "lon"), P("lat", "lon"), P("lat", "lon"), P(None, ("lon", "lat")))
    return jax.shard_map(shards, mesh=mesh, in_specs=in_specs, out_specs=out_specs, check_vma=False)
```

profile of v0, /device:TPU:0, one launch (start us, length us, event | category | flops | bytes accessed | tf_op | source)
XLA Modules:
  0.0 315.2 jit_solution(3378495073468807905)
XLA Ops:
  6.3 9.0 %reduce-window.14 = s32[32,8,128]{2,1,0:T(8,128)S(1)} reduce-window(s32[32,8,128]{2,1,0:T(8,128)S(1)} %fusion.46, s32[]{:T(128)} %constant.62.clone.1), window={size=1x1x128 pad=0_0x0_0x127_0}, to_apply=%region_0.0 | reduce-window | flops 4161536 | bytes 262148 | tf_op jit(solution)/shard_map/reduce-window
  45.2 6.2 %all-to-all-start.1 = ((f32[8,1,512]{2,1,0:T(1,128)}), f32[8,1,512]{2,1,0:T(1,128)S(1)}, u32[]{:S(2)}, u32[]{:S(2)}) async-start(f32[8,1,512]{2,1,0:T(1,128)} %reshape.275), calls=%async_computation.1 | async-start | bytes 32768 | tf_op jit(solution)/shard_map/all_to_all | solution.py:79
  52.4 5.6 %all-to-all-done.1 = f32[8,1,512]{2,1,0:T(1,128)S(1)} async-done(((f32[8,1,512]{2,1,0:T(1,128)}), f32[8,1,512]{2,1,0:T(1,128)S(1)}, u32[]{:S(2)}, u32[]{:S(2)}) %all-to-all-start.1) | async-done | bytes 16416 | tf_op jit(solution)/shard_map/all_to_all | solution.py:79
  62.2 13.8 %scatter_custom_fusion = f32[524288]{0:T(1024)} fusion(s32[2048]{0:T(1024)S(1)} %bitcast.187, f32[2048]{0:T(1024)S(1)} %reshape.224, f32[]{:T(128)} %constant.60.clone.1), kind=kCustom, calls=%fused_computation.24 | custom fusion | flops 2048 | bytes 2097156 | tf_op jit(solution)/shard_map/scatter-add | solution.py:88
  79.6 4.6 %all-to-all-start.4 = ((f32[4,8,16,1024]{3,2,1,0:T(8,128)}), f32[4,8,16,1024]{3,2,1,0:T(8,128)}, u32[]{:S(2)}, u32[]{:S(2)}) async-start(f32[4,8,16,1024]{3,2,1,0:T(8,128)} %bitcast.159), calls=%async_computation.4 | async-start | bytes 4194304 | tf_op jit(solution)/shard_map/all_to_all | solution.py:105
  104.5 18.6 %collective-permute-start.8 = (f32[2,256,1]{2,1,0:T(8,128)S(1)}, f32[2,256,1]{2,1,0:T(8,128)S(1)}, u32[]{:S(2)}, u32[]{:S(2)}) collective-permute-start(f32[2,256,1]{2,1,0:T(8,128)S(1)} %get-tuple-element.52), channel_id=1, source_target_pairs={{0,8},{8,16},{16,24},{1,9},{9,17},{17,25},{2,10},{10,18},{18,26},{... | collective-permute-start | bytes 6152 | tf_op jit(solution)/shard_map/ppermute | solution.py:26
  125.6 4.9 %collective-permute-start.10 = (f32[2,1,514]{2,1,0:T(1,128)S(1)}, f32[2,1,514]{2,1,0:T(1,128)S(1)}, u32[]{:S(2)}, u32[]{:S(2)}) collective-permute-start(f32[2,1,514]{2,1,0:T(1,128)S(1)} %get-tuple-element.36), channel_id=1, source_target_pairs={{0,1},{1,2},{2,3},{3,4},{4,5},{5,6},{6,7},{8,9},{9,10},{10,11},{11... | collective-permute-start | bytes 12344 | tf_op jit(solution)/shard_map/ppermute | solution.py:26
  135.5 5.0 %all-to-all-start.3 = ((f32[4,8,16]{2,0,1:T(4,128)}), f32[4,8,16]{2,0,1:T(4,128)S(1)}, u32[]{:S(2)}, u32[]{:S(2)}) async-start(f32[4,8,16]{2,0,1:T(4,128)} %copy.76), calls=%async_computation.3 | async-start | bytes 32768 | tf_op jit(solution)/shard_map/all_to_all | solution.py:111
  147.1 5.9 %all-to-all-start.5 = ((f32[4,8,16,1024]{3,2,0,1:T(8,128)}), f32[4,8,16,1024]{3,2,0,1:T(8,128)}, u32[]{:S(2)}, u32[]{:S(2)}) async-start(f32[4,8,16,1024]{3,2,0,1:T(8,128)} %copy.78), calls=%async_computation.5 | async-start | bytes 4194304 | tf_op jit(solution)/shard_map/all_to_all | solution.py:104
  158.4 6.1 %collective-permute-done.12 = f32[256,1]{1,0:T(8,128)S(1)} collective-permute-done((f32[256,1]{1,0:T(8,128)S(1)}, f32[256,1]{1,0:T(8,128)S(1)}, u32[]{:S(2)}, u32[]{:S(2)}) %collective-permute-start.12) | collective-permute-done | bytes 1056 | tf_op jit(solution)/shard_map/ppermute | solution.py:27
  175.9 5.5 %collective-permute-start.16 = (f32[2,256,1]{2,1,0:T(8,128)S(1)}, f32[2,256,1]{2,1,0:T(8,128)S(1)}, u32[]{:S(2)}, u32[]{:S(2)}) collective-permute-start(f32[2,256,1]{2,1,0:T(8,128)S(1)} %get-tuple-element.50), channel_id=1, source_target_pairs={{0,8},{8,16},{16,24},{1,9},{9,17},{17,25},{2,10},{10,18},{18,26},{... | collective-permute-start | bytes 6152 | tf_op jit(solution)/shard_map/ppermute | solution.py:26
  184.0 16.5 %collective-permute-start.18 = (f32[2,1,514]{2,1,0:T(1,128)S(1)}, f32[2,1,514]{2,1,0:T(1,128)S(1)}, u32[]{:S(2)}, u32[]{:S(2)}) collective-permute-start(f32[2,1,514]{2,1,0:T(1,128)S(1)} %get-tuple-element.34), channel_id=1, source_target_pairs={{0,1},{1,2},{2,3},{3,4},{4,5},{5,6},{6,7},{8,9},{9,10},{10,11},{11... | collective-permute-start | bytes 12344 | tf_op jit(solution)/shard_map/ppermute | solution.py:26
  204.1 5.1 %collective-permute-start.21 = (f32[256,1]{1,0:T(8,128)S(1)}, f32[256,1]{1,0:T(8,128)S(1)}, u32[]{:S(2)}, u32[]{:S(2)}) collective-permute-start(f32[256,1]{1,0:T(8,128)S(1)} %get-tuple-element.66), channel_id=1, source_target_pairs={{0,8},{8,16},{16,24},{1,9},{9,17},{17,25},{2,10},{10,18},{18,26},{... | collective-permute-start | bytes 3080 | tf_op jit(solution)/shard_map/ppermute | solution.py:26
  210.5 4.6 %collective-permute-done.20 = f32[256,1]{1,0:T(8,128)S(1)} collective-permute-done((f32[256,1]{1,0:T(8,128)S(1)}, f32[256,1]{1,0:T(8,128)S(1)}, u32[]{:S(2)}, u32[]{:S(2)}) %collective-permute-start.20) | collective-permute-done | bytes 1056 | tf_op jit(solution)/shard_map/ppermute | solution.py:27
  215.2 5.3 %collective-permute-start.23 = (f32[1,514]{1,0:T(1,128)S(1)}, f32[1,514]{1,0:T(1,128)S(1)}, u32[]{:S(2)}, u32[]{:S(2)}) collective-permute-start(f32[1,514]{1,0:T(1,128)S(1)} %get-tuple-element.59), channel_id=1, source_target_pairs={{0,1},{1,2},{2,3},{3,4},{4,5},{5,6},{6,7},{8,9},{9,10},{10,11},{11... | collective-permute-start | bytes 6176 | tf_op jit(solution)/shard_map/ppermute | solution.py:26
  221.9 14.3 %collective-permute-done.22 = f32[1,514]{1,0:T(1,128)S(1)} collective-permute-done((f32[1,514]{1,0:T(1,128)S(1)}, f32[1,514]{1,0:T(1,128)S(1)}, u32[]{:S(2)}, u32[]{:S(2)}) %collective-permute-start.22) | collective-permute-done | bytes 2088 | tf_op jit(solution)/shard_map/ppermute | solution.py:27
  238.1 4.9 %collective-permute-start.24 = (f32[2,256,1]{2,1,0:T(8,128)S(1)}, f32[2,256,1]{2,1,0:T(8,128)S(1)}, u32[]{:S(2)}, u32[]{:S(2)}) collective-permute-start(f32[2,256,1]{2,1,0:T(8,128)S(1)} %get-tuple-element.48), channel_id=1, source_target_pairs={{0,8},{8,16},{16,24},{1,9},{9,17},{17,25},{2,10},{10,18},{18,26},{... | collective-permute-start | bytes 6152 | tf_op jit(solution)/shard_map/ppermute | solution.py:26
  245.6 5.4 %collective-permute-start.26 = (f32[2,1,514]{2,1,0:T(1,128)S(1)}, f32[2,1,514]{2,1,0:T(1,128)S(1)}, u32[]{:S(2)}, u32[]{:S(2)}) collective-permute-start(f32[2,1,514]{2,1,0:T(1,128)S(1)} %get-tuple-element.32), channel_id=1, source_target_pairs={{0,1},{1,2},{2,3},{3,4},{4,5},{5,6},{6,7},{8,9},{9,10},{10,11},{11... | collective-permute-start | bytes 12344 | tf_op jit(solution)/shard_map/ppermute | solution.py:26
  256.7 5.8 %collective-permute-start.29 = (f32[256,1]{1,0:T(8,128)S(1)}, f32[256,1]{1,0:T(8,128)S(1)}, u32[]{:S(2)}, u32[]{:S(2)}) collective-permute-start(f32[256,1]{1,0:T(8,128)S(1)} %get-tuple-element.65), channel_id=1, source_target_pairs={{0,8},{8,16},{16,24},{1,9},{9,17},{17,25},{2,10},{10,18},{18,26},{... | collective-permute-start | bytes 3080 | tf_op jit(solution)/shard_map/ppermute | solution.py:26
  273.9 5.1 %collective-permute-start.31 = (f32[1,514]{1,0:T(1,128)S(1)}, f32[1,514]{1,0:T(1,128)S(1)}, u32[]{:S(2)}, u32[]{:S(2)}) collective-permute-start(f32[1,514]{1,0:T(1,128)S(1)} %get-tuple-element.57), channel_id=1, source_target_pairs={{0,1},{1,2},{2,3},{3,4},{4,5},{5,6},{6,7},{8,9},{9,10},{10,11},{11... | collective-permute-start | bytes 6176 | tf_op jit(solution)/shard_map/ppermute | solution.py:26
  280.3 4.9 %fusion.3 = (f32[4,8,16]{2,0,1:T(4,128)S(1)}, f32[4,8,16]{2,0,1:T(4,128)S(1)}, f32[4,8,16]{2,0,1:T(4,128)S(1)}, f32[4,8,16]{2,0,1:T(4,128)S(1)}) fusion(f32[4,8,16,1024]{3,2,0,1:T(8,128)} %all-to-all-done.5, f32[4,8,16,1024]{3,2,1,0:T(8,128)} %bitcast.163, f32[4,8,16,1024]{3,2,1,0:T(8,128)} %bitcast.160, f32[4,8,16,1024]{3,2,1,0:T(8,128)} %bitcast.161, ...), kind=kLoop, calls=%fused_computation.17 | loop fusion | flops 4192256 | bytes 10493952 | tf_op jit(solution)/shard_map/reduce_sum | solution.py:131
  285.9 4.7 %all-to-all-start.6 = ((f32[4,1,512]{2,1,0:T(1,128)}), f32[4,1,512]{2,1,0:T(1,128)S(1)}, u32[]{:S(2)}, u32[]{:S(2)}) async-start(f32[4,1,512]{2,1,0:T(1,128)} %reshape.279), calls=%async_computation.6 | async-start | bytes 16384 | tf_op jit(solution)/shard_map/all_to_all | solution.py:134
  296.0 10.1 %all-to-all-start.7 = ((f32[8,1,256]{2,1,0:T(1,128)}), f32[8,1,256]{2,1,0:T(1,128)S(1)}, u32[]{:S(2)}, u32[]{:S(2)}) async-start(f32[8,1,256]{2,1,0:T(1,128)} %reshape.281), calls=%async_computation.7 | async-start | bytes 16384 | tf_op jit(solution)/shard_map/all_to_all | solution.py:133
  307.5 5.0 %all-to-all-done.7 = f32[8,1,256]{2,1,0:T(1,128)S(1)} async-done(((f32[8,1,256]{2,1,0:T(1,128)}), f32[8,1,256]{2,1,0:T(1,128)S(1)}, u32[]{:S(2)}, u32[]{:S(2)}) %all-to-all-start.7) | async-done | bytes 8224 | tf_op jit(solution)/shard_map/all_to_all | solution.py:133
  (217 shorter events, 136.4 us)
Async XLA Ops:
  1.9 29.1 %collective-permute-start.1 = (f32[2,256,1]{2,1,0:T(8,128)S(1)}, f32[2,256,1]{2,1,0:T(8,128)S(1)}, u32[]{:S(2)}, u32[]{:S(2)}) collective-permute-start(f32[2,256,1]{2,1,0:T(8,128)S(1)} %get-tuple-element.55), channel_id=1, source_target_pairs={{8,0},{16,8},{24,16},{9,1},{17,9},{25,17},{10,2},{18,10},{26,18},{... | collective-permute-start | bytes 6152 | tf_op jit(solution)/shard_map/ppermute | solution.py:27
  3.2 27.8 %collective-permute-start = (f32[2,256,1]{2,1,0:T(8,128)S(1)}, f32[2,256,1]{2,1,0:T(8,128)S(1)}, u32[]{:S(2)}, u32[]{:S(2)}) collective-permute-start(f32[2,256,1]{2,1,0:T(8,128)S(1)} %get-tuple-element.54), channel_id=1, source_target_pairs={{0,8},{8,16},{16,24},{1,9},{9,17},{17,25},{2,10},{10,18},{18,26},{... | collective-permute-start | bytes 6152 | tf_op jit(solution)/shard_map/ppermute | solution.py:26
  25.8 17.5 %all-to-all-start = ((f32[4,1,1024]{2,1,0:T(1,128)}), f32[4,1,1024]{2,1,0:T(1,128)S(1)}, u32[]{:S(2)}, u32[]{:S(2)}) async-start(f32[4,1,1024]{2,1,0:T(1,128)} %reshape.273), calls=%async_computation | async-start | bytes 32768 | tf_op jit(solution)/shard_map/all_to_all | solution.py:80
  31.1 11.6 %collective-permute-start.3 = (f32[2,1,514]{2,1,0:T(1,128)S(1)}, f32[2,1,514]{2,1,0:T(1,128)S(1)}, u32[]{:S(2)}, u32[]{:S(2)}) collective-permute-start(f32[2,1,514]{2,1,0:T(1,128)S(1)} %get-tuple-element.39), channel_id=1, source_target_pairs={{1,0},{2,1},{3,2},{4,3},{5,4},{6,5},{7,6},{9,8},{10,9},{11,10},{12... | collective-permute-start | bytes 12344 | tf_op jit(solution)/shard_map/ppermute | solution.py:27
  32.4 10.3 %collective-permute-start.2 = (f32[2,1,514]{2,1,0:T(1,128)S(1)}, f32[2,1,514]{2,1,0:T(1,128)S(1)}, u32[]{:S(2)}, u32[]{:S(2)}) collective-permute-start(f32[2,1,514]{2,1,0:T(1,128)S(1)} %get-tuple-element.38), channel_id=1, source_target_pairs={{0,1},{1,2},{2,3},{3,4},{4,5},{5,6},{6,7},{8,9},{9,10},{10,11},{11... | collective-permute-start | bytes 12344 | tf_op jit(solution)/shard_map/ppermute | solution.py:26
  45.2 12.8 %all-to-all-start.1 = ((f32[8,1,512]{2,1,0:T(1,128)}), f32[8,1,512]{2,1,0:T(1,128)S(1)}, u32[]{:S(2)}, u32[]{:S(2)}) async-start(f32[8,1,512]{2,1,0:T(1,128)} %reshape.275), calls=%async_computation.1 | async-start | bytes 32768 | tf_op jit(solution)/shard_map/all_to_all | solution.py:79
  58.0 21.6 %all-to-all-start.2 = ((f32[4,1,128]{2,1,0:T(1,128)}), f32[4,1,128]{2,1,0:T(1,128)S(1)}, u32[]{:S(2)}, u32[]{:S(2)}) async-start(f32[4,1,128]{2,1,0:T(1,128)} %reshape.277), calls=%async_computation.2 | async-start | bytes 4096 | tf_op jit(solution)/shard_map/all_to_all | solution.py:112
  79.6 55.9 %all-to-all-start.4 = ((f32[4,8,16,1024]{3,2,1,0:T(8,128)}), f32[4,8,16,1024]{3,2,1,0:T(8,128)}, u32[]{:S(2)}, u32[]{:S(2)}) async-start(f32[4,8,16,1024]{3,2,1,0:T(8,128)} %bitcast.159), calls=%async_computation.4 | async-start | bytes 4194304 | tf_op jit(solution)/shard_map/all_to_all | solution.py:105
  103.2 19.9 %collective-permute-start.9 = (f32[2,256,1]{2,1,0:T(8,128)S(1)}, f32[2,256,1]{2,1,0:T(8,128)S(1)}, u32[]{:S(2)}, u32[]{:S(2)}) collective-permute-start(f32[2,256,1]{2,1,0:T(8,128)S(1)} %get-tuple-element.53), channel_id=1, source_target_pairs={{8,0},{16,8},{24,16},{9,1},{17,9},{25,17},{10,2},{18,10},{26,18},{... | collective-permute-start | bytes 6152 | tf_op jit(solution)/shard_map/ppermute | solution.py:27
  104.5 19.7 %collective-permute-start.8 = (f32[2,256,1]{2,1,0:T(8,128)S(1)}, f32[2,256,1]{2,1,0:T(8,128)S(1)}, u32[]{:S(2)}, u32[]{:S(2)}) collective-permute-start(f32[2,256,1]{2,1,0:T(8,128)S(1)} %get-tuple-element.52), channel_id=1, source_target_pairs={{0,8},{8,16},{16,24},{1,9},{9,17},{17,25},{2,10},{10,18},{18,26},{... | collective-permute-start | bytes 6152 | tf_op jit(solution)/shard_map/ppermute | solution.py:26
  124.3 8.5 %collective-permute-start.11 = (f32[2,1,514]{2,1,0:T(1,128)S(1)}, f32[2,1,514]{2,1,0:T(1,128)S(1)}, u32[]{:S(2)}, u32[]{:S(2)}) collective-permute-start(f32[2,1,514]{2,1,0:T(1,128)S(1)} %get-tuple-element.37), channel_id=1, source_target_pairs={{1,0},{2,1},{3,2},{4,3},{5,4},{6,5},{7,6},{9,8},{10,9},{11,10},{12... | collective-permute-start | bytes 12344 | tf_op jit(solution)/shard_map/ppermute | solution.py:27
  135.5 11.6 %all-to-all-start.3 = ((f32[4,8,16]{2,0,1:T(4,128)}), f32[4,8,16]{2,0,1:T(4,128)S(1)}, u32[]{:S(2)}, u32[]{:S(2)}) async-start(f32[4,8,16]{2,0,1:T(4,128)} %copy.76), calls=%async_computation.3 | async-start | bytes 32768 | tf_op jit(solution)/shard_map/all_to_all | solution.py:111
  147.1 133.2 %all-to-all-start.5 = ((f32[4,8,16,1024]{3,2,0,1:T(8,128)}), f32[4,8,16,1024]{3,2,0,1:T(8,128)}, u32[]{:S(2)}, u32[]{:S(2)}) async-start(f32[4,8,16,1024]{3,2,0,1:T(8,128)} %copy.78), calls=%async_computation.5 | async-start | bytes 4194304 | tf_op jit(solution)/shard_map/all_to_all | solution.py:104
  157.0 7.4 %collective-permute-start.12 = (f32[256,1]{1,0:T(8,128)S(1)}, f32[256,1]{1,0:T(8,128)S(1)}, u32[]{:S(2)}, u32[]{:S(2)}) collective-permute-start(f32[256,1]{1,0:T(8,128)S(1)} %get-tuple-element.69), channel_id=1, source_target_pairs={{8,0},{16,8},{24,16},{9,1},{17,9},{25,17},{10,2},{18,10},{26,18},{... | collective-permute-start | bytes 3080 | tf_op jit(solution)/shard_map/ppermute | solution.py:27
  182.7 18.7 %collective-permute-start.19 = (f32[2,1,514]{2,1,0:T(1,128)S(1)}, f32[2,1,514]{2,1,0:T(1,128)S(1)}, u32[]{:S(2)}, u32[]{:S(2)}) collective-permute-start(f32[2,1,514]{2,1,0:T(1,128)S(1)} %get-tuple-element.35), channel_id=1, source_target_pairs={{1,0},{2,1},{3,2},{4,3},{5,4},{6,5},{7,6},{9,8},{10,9},{11,10},{12... | collective-permute-start | bytes 12344 | tf_op jit(solution)/shard_map/ppermute | solution.py:27
  184.0 17.8 %collective-permute-start.18 = (f32[2,1,514]{2,1,0:T(1,128)S(1)}, f32[2,1,514]{2,1,0:T(1,128)S(1)}, u32[]{:S(2)}, u32[]{:S(2)}) collective-permute-start(f32[2,1,514]{2,1,0:T(1,128)S(1)} %get-tuple-element.34), channel_id=1, source_target_pairs={{0,1},{1,2},{2,3},{3,4},{4,5},{5,6},{6,7},{8,9},{9,10},{10,11},{11... | collective-permute-start | bytes 12344 | tf_op jit(solution)/shard_map/ppermute | solution.py:26
  220.6 15.6 %collective-permute-start.22 = (f32[1,514]{1,0:T(1,128)S(1)}, f32[1,514]{1,0:T(1,128)S(1)}, u32[]{:S(2)}, u32[]{:S(2)}) collective-permute-start(f32[1,514]{1,0:T(1,128)S(1)} %get-tuple-element.58), channel_id=1, source_target_pairs={{1,0},{2,1},{3,2},{4,3},{5,4},{6,5},{7,6},{9,8},{10,9},{11,10},{12... | collective-permute-start | bytes 6176 | tf_op jit(solution)/shard_map/ppermute | solution.py:27
  244.3 7.7 %collective-permute-start.27 = (f32[2,1,514]{2,1,0:T(1,128)S(1)}, f32[2,1,514]{2,1,0:T(1,128)S(1)}, u32[]{:S(2)}, u32[]{:S(2)}) collective-permute-start(f32[2,1,514]{2,1,0:T(1,128)S(1)} %get-tuple-element.33), channel_id=1, source_target_pairs={{1,0},{2,1},{3,2},{4,3},{5,4},{6,5},{7,6},{9,8},{10,9},{11,10},{12... | collective-permute-start | bytes 12344 | tf_op jit(solution)/shard_map/ppermute | solution.py:27
  255.4 18.4 %collective-permute-start.28 = (f32[256,1]{1,0:T(8,128)S(1)}, f32[256,1]{1,0:T(8,128)S(1)}, u32[]{:S(2)}, u32[]{:S(2)}) collective-permute-start(f32[256,1]{1,0:T(8,128)S(1)} %get-tuple-element.64), channel_id=1, source_target_pairs={{8,0},{16,8},{24,16},{9,1},{17,9},{25,17},{10,2},{18,10},{26,18},{... | collective-permute-start | bytes 3080 | tf_op jit(solution)/shard_map/ppermute | solution.py:27
  256.7 17.1 %collective-permute-start.29 = (f32[256,1]{1,0:T(8,128)S(1)}, f32[256,1]{1,0:T(8,128)S(1)}, u32[]{:S(2)}, u32[]{:S(2)}) collective-permute-start(f32[256,1]{1,0:T(8,128)S(1)} %get-tuple-element.65), channel_id=1, source_target_pairs={{0,8},{8,16},{16,24},{1,9},{9,17},{17,25},{2,10},{10,18},{18,26},{... | collective-permute-start | bytes 3080 | tf_op jit(solution)/shard_map/ppermute | solution.py:26
  273.9 32.2 %collective-permute-start.31 = (f32[1,514]{1,0:T(1,128)S(1)}, f32[1,514]{1,0:T(1,128)S(1)}, u32[]{:S(2)}, u32[]{:S(2)}) collective-permute-start(f32[1,514]{1,0:T(1,128)S(1)} %get-tuple-element.57), channel_id=1, source_target_pairs={{0,1},{1,2},{2,3},{3,4},{4,5},{5,6},{6,7},{8,9},{9,10},{10,11},{11... | collective-permute-start | bytes 6176 | tf_op jit(solution)/shard_map/ppermute | solution.py:26
  279.0 27.1 %collective-permute-start.30 = (f32[1,514]{1,0:T(1,128)S(1)}, f32[1,514]{1,0:T(1,128)S(1)}, u32[]{:S(2)}, u32[]{:S(2)}) collective-permute-start(f32[1,514]{1,0:T(1,128)S(1)} %get-tuple-element.56), channel_id=1, source_target_pairs={{1,0},{2,1},{3,2},{4,3},{5,4},{6,5},{7,6},{9,8},{10,9},{11,10},{12... | collective-permute-start | bytes 6176 | tf_op jit(solution)/shard_map/ppermute | solution.py:27
  285.9 8.5 %all-to-all-start.6 = ((f32[4,1,512]{2,1,0:T(1,128)}), f32[4,1,512]{2,1,0:T(1,128)S(1)}, u32[]{:S(2)}, u32[]{:S(2)}) async-start(f32[4,1,512]{2,1,0:T(1,128)} %reshape.279), calls=%async_computation.6 | async-start | bytes 16384 | tf_op jit(solution)/shard_map/all_to_all | solution.py:134
  296.0 16.6 %all-to-all-start.7 = ((f32[8,1,256]{2,1,0:T(1,128)}), f32[8,1,256]{2,1,0:T(1,128)S(1)}, u32[]{:S(2)}, u32[]{:S(2)}) async-start(f32[8,1,256]{2,1,0:T(1,128)} %reshape.281), calls=%async_computation.7 | async-start | bytes 16384 | tf_op jit(solution)/shard_map/all_to_all | solution.py:133
  (38 other events, 344.6 us)
where the time goes:
time: 317 us; the launch traced here: 315 us
  starting transfers between devices  163 us (51%)
  waiting for transfers between devices  54.5 us (17%)
  other arithmetic  48.5 us (15%)
  local copies, waits for them, and re-layouts  46.2 us (15%)
    ppermute x16, starting transfers between devices, padded_2(): before = lax.ppermute(last, axis, up)  98.8 us
    ppermute x16, waiting for transfers between devices, padded_2(): after = lax.ppermute(first, axis, down)  35.8 us
    ppermute x16, starting transfers between devices, padded_2(): after = lax.ppermute(first, axis, down)  20.7 us
    unnamed x60, local copies, waits for them, and re-layouts  15.2 us
    scatter-add x1, other arithmetic, shards(): forcing = jnp.zeros((ITERS * cells,), jnp.float32).at[landing].add(amounts)  13.8 us
    gather x4, local copies, waits for them, and re-layouts, shards(): tile_blocks(height)[held_index] * held_feet  10.8 us
    all_to_all x1, starting transfers between devices, shards(): lax.all_to_all(lax.all_to_all(collected, 'lon', split_axis=0, concat_axis...  10.1 us
    another operation x5, other arithmetic  9.78 us
  transfers between devices with their start and end apart: 40, of which 15 were waited for; matrix products, arithmetic and copies ran while one was open for 28% of the time, Pallas kernels for 0%

commit v1 on v0

v1 whole, which is shorter than its diff:
```python
import functools

import jax
import jax.numpy as jnp
from jax import lax
from jax.experimental import pallas as pl
from jax.experimental.pallas import tpu as pltpu
from jax.sharding import PartitionSpec as P

ITERS = 4
STA_DEV = 256
SRC_DEV = 20
BH = 8
BW = 128
EDGE = 2 * ITERS
LANES = 128
FIELDS = 4 + ITERS

GRAVITY_STEP = 0.8
DEPTH_STEP = 0.8
TURN_RATE = 0.1
RETAIN = 0.97

MESH = pl.DeviceIdType.MESH
F32 = jnp.float32
BF16 = jnp.bfloat16


def split(values):
    high = values.astype(BF16)
    return high, (values - high.astype(F32)).astype(BF16)


def rolled(values, shift, axis):
    return pltpu.roll(values, shift % values.shape[axis], axis)


def central(values, axis):
    return rolled(values, -1, axis) - rolled(values, 1, axis)


def nt_dot(left, right):
    return lax.dot_general(left, right, (((1,), (1,)), ((), ())), preferred_element_type=F32)


def kernel(
    lon_count,
    lat_count,
    limit,
    eta_ref,
    east_ref,
    north_ref,
    depth_ref,
    packet_ref,
    feet_ref,
    eta_out,
    east_out,
    north_out,
    back_out,
    arrived,
    held,
    ext,
    to_east,
    to_west,
    from_west,
    from_east,
    blocks,
    partial,
    sta_send,
    sta_recv,
    foot_send,
    foot_recv,
    back_send,
    back_recv,
    edge_send,
    edge_recv,
):
    lon = lax.axis_index("lon")
    lat = lax.axis_index("lat")
    devices = lon_count * lat_count
    me = lon * lat_count + lat
    rows, cols = eta_ref.shape
    tail = cols
    wide = cols + LANES
    tall = rows + 2 * EDGE
    slots = devices * limit
    group = partial.shape[0]
    per_group = devices // group

    def peer(i):
        return lax.rem(me + i, devices)

    def place(d):
        return (d // lat_count, lax.rem(d, lat_count))

    barrier = pltpu.get_barrier_semaphore()

    @pl.loop(1, devices)
    def _(i):
        pl.semaphore_signal(barrier, inc=1, device_id=place(peer(i)), device_id_type=MESH)

    pl.semaphore_wait(barrier, devices - 1)

    def sta_copy(to, slot):
        return pltpu.make_async_remote_copy(
            src_ref=packet_ref.at[to],
            dst_ref=arrived.at[slot],
            send_sem=sta_send.at[to],
            recv_sem=sta_recv.at[slot],
            device_id=place(to),
            device_id_type=MESH,
        )

    def foot_copy(to, slot):
        return pltpu.make_async_remote_copy(
            src_ref=feet_ref.at[pl.ds(pl.multiple_of(to * limit, 8), limit)],
            dst_ref=held.at[pl.ds(pl.multiple_of(slot * limit, 8), limit)],
            send_sem=foot_send.at[to],
            recv_sem=foot_recv.at[slot],
            device_id=place(to),
            device_id_type=MESH,
        )

    def back_copy(to, slot):
        return pltpu.make_async_remote_copy(
            src_ref=partial.at[to // per_group],
            dst_ref=back_out.at[slot],
            send_sem=back_send.at[to],
            recv_sem=back_recv.at[slot],
            device_id=place(to),
            device_id_type=MESH,
        )

    def start_feet(low, high):
        @pl.loop(low, high)
        def _(i):
            foot_copy(peer(i), me).start()

    @pl.loop(1, devices)
    def _(i):
        sta_copy(peer(i), me).start()

    first = 1 + devices // 4
    second = first + devices // 8
    start_feet(1, first)

    arrived[me] = packet_ref[me]
    own = pl.ds(pl.multiple_of(me * limit, 8), limit)
    held[own] = feet_ref[own]
    for field, ref in enumerate((eta_ref, east_ref, north_ref, depth_ref)):
        ext[field, :rows, :cols] = ref[...]
    for k in range(ITERS):
        ext[4 + k, :rows, :cols] = jnp.zeros((rows, cols), F32)

    @pl.loop(1, devices)
    def _(i):
        sta_copy(me, peer(i)).wait_recv()

    width = packet_ref.shape[2]
    bunch = 4
    high_lane = lax.rem(lax.broadcasted_iota(jnp.int32, (1, bunch * width), 1), width) < width // 2
    row_id = lax.broadcasted_iota(jnp.int32, (rows, bunch * width), 0).astype(F32)
    col_id = lax.broadcasted_iota(jnp.int32, (cols, bunch * width), 0).astype(F32)

    @pl.loop(0, devices // bunch)
    def _(g):
        def line(q):
            return jnp.concatenate(
                [arrived[g * bunch + j, q : q + 1, :] for j in range(bunch)], axis=1
            )

        amount, at_row, at_col = line(0), line(1), line(2)
        high = amount.astype(BF16).astype(F32)
        piece = jnp.where(high_lane, high, amount - high)
        right = jnp.where(col_id == at_col, piece, 0.0).astype(BF16)
        for k in range(ITERS):
            left = jnp.where(row_id == at_row - k * rows, 1.0, 0.0).astype(BF16)
            ext[4 + k, :rows, :cols] += nt_dot(left, right)

    lane = lax.broadcasted_iota(jnp.int32, (rows, LANES), 1)

    def strip(low, start):
        out = jnp.zeros((rows, LANES), F32)
        for field in range(FIELDS):
            tile = ext[field, :rows, low : low + LANES]
            moved = rolled(tile, EDGE * field - start, 1)
            inside = (lane >= EDGE * field) & (lane < EDGE * (field + 1))
            out = jnp.where(inside, moved, out)
        return out

    to_east[...] = strip(cols - LANES, LANES - EDGE)
    to_west[...] = strip(0, 0)

    def edge_copy(src, dst, number, to):
        return pltpu.make_async_remote_copy(
            src_ref=src,
            dst_ref=dst,
            send_sem=edge_send.at[number],
            recv_sem=edge_recv.at[number],
            device_id=to,
            device_id_type=MESH,
        )

    has_west, has_east = lon > 0, lon < lon_count - 1
    has_north, has_south = lat > 0, lat < lat_count - 1
    east_copy = edge_copy(to_east, from_west, 0, (lax.rem(lon + 1, lon_count), lat))
    west_copy = edge_copy(to_west, from_east, 1, (lax.rem(lon + lon_count - 1, lon_count), lat))
    south_copy = edge_copy(
        ext.at[:, rows - EDGE : rows, :],
        ext.at[:, rows + EDGE : tall, :],
        2,
        (lon, lax.rem(lat + 1, lat_count)),
    )
    north_copy = edge_copy(
        ext.at[:, 0:EDGE, :],
        ext.at[:, rows : rows + EDGE, :],
        3,
        (lon, lax.rem(lat + lat_count - 1, lat_count)),
    )

    pl.when(has_east)(east_copy.start)
    pl.when(has_west)(west_copy.start)
    start_feet(first, second)

    @pl.when(lon == 0)
    def _():
        from_west[...] = jnp.zeros((rows, LANES), F32)

    @pl.when(lon == lon_count - 1)
    def _():
        from_east[...] = jnp.zeros((rows, LANES), F32)

    pl.when(has_west)(east_copy.wait_recv)
    pl.when(has_east)(west_copy.wait_recv)
    for field in range(FIELDS):
        after = rolled(from_east[...], -EDGE * field, 1)
        before = rolled(from_west[...], LANES - EDGE - EDGE * field, 1)
        ext[field, :rows, tail:] = jnp.where(
            lane < EDGE, after, jnp.where(lane >= LANES - EDGE, before, 0.0)
        )

    pl.when(has_south)(south_copy.start)
    pl.when(has_north)(north_copy.start)
    start_feet(second, devices)

    @pl.when(lat == 0)
    def _():
        ext[:, rows + EDGE : tall, :] = jnp.zeros((FIELDS, EDGE, wide), F32)

    @pl.when(lat == lat_count - 1)
    def _():
        ext[:, rows : rows + EDGE, :] = jnp.zeros((FIELDS, EDGE, wide), F32)

    pl.when(has_north)(south_copy.wait_recv)
    pl.when(has_south)(north_copy.wait_recv)
    pl.when(has_east)(east_copy.wait_send)
    pl.when(has_west)(west_copy.wait_send)
    pl.when(has_south)(south_copy.wait_send)
    pl.when(has_north)(north_copy.wait_send)

    at_row = lax.broadcasted_iota(jnp.int32, (tall, wide), 0)
    at_col = lax.broadcasted_iota(jnp.int32, (tall, wide), 1)
    row_end = rows + jnp.where(has_south, EDGE, 0)
    row_begin = tall - jnp.where(has_north, EDGE, 0)
    col_end = cols + jnp.where(has_east, EDGE, 0)
    col_begin = wide - jnp.where(has_west, EDGE, 0)
    inside = ((at_row < row_end) | (at_row >= row_begin)) & (
        (at_col < col_end) | (at_col >= col_begin)
    )
    mask = jnp.where(inside, 1.0, 0.0)

    bands = rows // BH
    block_cols = cols // BW
    count = bands * block_cols
    for period in range(ITERS - 1, -1, -1):
        east, north = ext[1], ext[2]
        pressure = (
            ext[0] + ext[4 + period] - 0.5 * GRAVITY_STEP * (central(east, 1) + central(north, 0))
        )
        ext[0] = pressure
        flux = ext[3] * pressure
        ext[1] = mask * (
            RETAIN * east + TURN_RATE * north - 0.5 * DEPTH_STEP * central(flux, 1)
        )
        ext[2] = mask * (
            RETAIN * north - TURN_RATE * east - 0.5 * DEPTH_STEP * central(flux, 0)
        )
        for c in range(block_cols):
            tiles = ext[0, :rows, c * BW : (c + 1) * BW].reshape(bands, BH, BW)
            for r in range(BH):
                low = period * count + c * bands
                blocks[low : low + bands, r * BW : (r + 1) * BW] = tiles[:, r, :]

    eta_out[...] = ext[0, :rows, :cols]
    east_out[...] = ext[1, :rows, :cols]
    north_out[...] = ext[2, :rows, :cols]

    ids = jnp.sum(arrived[:, 4 : 4 + group, :], axis=0)
    block_high, block_low = split(blocks[...])
    number = lax.broadcasted_iota(jnp.int32, (count, LANES), 0)
    number = (lax.rem(number, bands) * block_cols + number // bands).astype(F32)

    @pl.loop(1, devices)
    def _(i):
        foot_copy(me, peer(i)).wait_recv()

    for g in range(group):
        foot_high, foot_low = split(held[g * LANES : (g + 1) * LANES, :])
        both = (
            nt_dot(block_high, foot_high)
            + nt_dot(block_high, foot_low)
            + nt_dot(block_low, foot_high)
        )
        wanted = number == ids[g : g + 1, :]
        for k in range(ITERS):
            found = jnp.where(wanted, both[k * count : (k + 1) * count], 0.0)
            partial[g, k : k + 1, :] = jnp.sum(found, axis=0, keepdims=True)
        partial[g, ITERS:, :] = jnp.zeros((8 - ITERS, LANES), F32)

    @pl.loop(1, devices)
    def _(i):
        back_copy(peer(i), me).start()

    back_out[me] = partial[me // per_group]

    @pl.loop(1, devices)
    def _(i):
        sta_copy(peer(i), me).wait_send()
        foot_copy(peer(i), me).wait_send()
        back_copy(peer(i), me).wait_send()
        back_copy(me, peer(i)).wait_recv()


def ranks(one_hot):
    size = one_hot.shape[0]
    at = jnp.arange(size, dtype=jnp.int32)
    lower = (at[:, None] > at[None, :]).astype(BF16)
    before = jnp.dot(lower, one_hot.astype(BF16), preferred_element_type=F32)
    return jnp.sum(before * one_hot, axis=1)


def exact_dot(left, right):
    return jnp.dot(left, right, precision=lax.Precision.HIGHEST, preferred_element_type=F32)


def shards(
    lon_count,
    lat_count,
    eta_adj,
    east_adj,
    north_adj,
    depth,
    station_owner,
    station_cell,
    station_misfit,
    footprints,
    foot_tile,
    foot_block,
    foot_source,
):
    devices = lon_count * lat_count
    rows, cols = eta_adj.shape
    records = station_cell.shape[0]
    feet = footprints.shape[0]
    capacity = max(2, 2 * records // devices)
    width = max(LANES, 2 * capacity)
    limit = max(8, 2 * feet // devices)
    slots = devices * limit
    group = slots // LANES
    me = lax.axis_index("lon") * lat_count + lax.axis_index("lat")
    names = jnp.arange(devices, dtype=jnp.int32)

    owner_hot = (station_owner == names[None, :]).astype(F32)
    rank = ranks(owner_hot)
    lanes = (jnp.arange(width, dtype=jnp.int32) % (width // 2)).astype(F32)
    slot_hot = (rank[:, None] == lanes[None, :]).astype(F32)
    period = jnp.arange(records, dtype=jnp.int32) // STA_DEV
    at_row = (period * rows + station_cell // cols).astype(F32)
    at_col = (station_cell % cols).astype(F32)
    spread = jnp.concatenate(
        [slot_hot * v[:, None] for v in (station_misfit, at_row, at_col)], axis=1
    )
    stations = exact_dot(owner_hot.T, spread).reshape(devices, 3, width)

    tile_hot = (foot_tile == names[None, :]).astype(F32)
    foot_place = foot_tile[:, 0] * limit + ranks(tile_hot).astype(jnp.int32)
    place_hot = (jnp.arange(slots, dtype=jnp.int32)[:, None] == foot_place[None, :]).astype(F32)
    foot_buffer = exact_dot(place_hot, footprints)
    ids = jnp.sum(place_hot * foot_block.astype(F32)[None, :], axis=1).reshape(devices, 1, limit)
    mine = (names == me).astype(F32)
    ids = (ids * mine[None, :, None]).reshape(devices, group, LANES)
    if width > LANES:
        ids = jnp.pad(ids, ((0, 0), (0, 0), (0, width - LANES)))
    packet = jnp.concatenate([stations, jnp.zeros((devices, 1, width), F32), ids], axis=1)
    depth_of = packet.shape[1]
    packet = jnp.pad(packet, ((0, 0), (0, -depth_of % 8), (0, 0)))
    depth_of = packet.shape[1]

    source_hot = (foot_source[:, None] == jnp.arange(SRC_DEV, dtype=jnp.int32)[None, :]).astype(F32)
    source_of = exact_dot(place_hot, source_hot)

    tall, wide = rows + 2 * EDGE, cols + LANES
    count = (rows // BH) * (cols // BW)
    vmem = pl.BlockSpec(memory_space=pltpu.VMEM)
    field = jax.ShapeDtypeStruct((rows, cols), F32)
    eta, east, north, back = pl.pallas_call(
        functools.partial(kernel, lon_count, lat_count, limit),
        out_shape=(field, field, field, jax.ShapeDtypeStruct((devices, 8, LANES), F32)),
        in_specs=[vmem] * 6,
        out_specs=(vmem,) * 4,
        scratch_shapes=[
            pltpu.VMEM((devices, depth_of, width), F32),
            pltpu.VMEM((slots, BH * BW), F32),
            pltpu.VMEM((FIELDS, tall, wide), F32),
            pltpu.VMEM((rows, LANES), F32),
            pltpu.VMEM((rows, LANES), F32),
            pltpu.VMEM((rows, LANES), F32),
            pltpu.VMEM((rows, LANES), F32),
            pltpu.VMEM((ITERS * count, BH * BW), F32),
            pltpu.VMEM((group, 8, LANES), F32),
            pltpu.SemaphoreType.DMA((devices,)),
            pltpu.SemaphoreType.DMA((devices,)),
            pltpu.SemaphoreType.DMA((devices,)),
            pltpu.SemaphoreType.DMA((devices,)),
            pltpu.SemaphoreType.DMA((devices,)),
            pltpu.SemaphoreType.DMA((devices,)),
            pltpu.SemaphoreType.DMA((4,)),
            pltpu.SemaphoreType.DMA((4,)),
        ],
        compiler_params=pltpu.CompilerParams(
            collective_id=0, has_side_effects=True, vmem_limit_bytes=60 * 1024 * 1024
        ),
    )(eta_adj, east_adj, north_adj, depth, packet, foot_buffer)

    start = lax.rem(me, devices // group) * limit
    mine_back = lax.dynamic_slice(back, (0, 0, start), (devices, ITERS, limit))
    by_slot = mine_back.transpose(1, 0, 2).reshape(ITERS, slots)
    uplift_grad = exact_dot(by_slot, source_of)
    return eta, east, north, uplift_grad


def solution(mesh):
    in_specs = (
        P("lat", "lon"),
        P("lat", "lon"),
        P("lat", "lon"),
        P("lat", "lon"),
        P(("lon", "lat"), None),
        P(("lon", "lat")),
        P(("lon", "lat")),
        P(("lon", "lat"), None),
        P(("lon", "lat"), None),
        P(("lon", "lat")),
        P(("lon", "lat")),
    )
    out_specs = (P("lat", "lon"), P("lat", "lon"), P("lat", "lon"), P(None, ("lon", "lat")))
    body = functools.partial(shards, mesh.shape["lon"], mesh.shape["lat"])
    return jax.shard_map(body, mesh=mesh, in_specs=in_specs, out_specs=out_specs, check_vma=False)
```

time: 317 us -> 93.4 us (0.29)
  starting transfers between devices: 163 us -> 0 us
  Pallas kernels: 0 us -> 78.4 us
  waiting for transfers between devices: 54.5 us -> 0 us
  other arithmetic: 48.5 us -> 3 us
  local copies, waits for them, and re-layouts: 46.2 us -> 5.23 us
  matrix products: 0.88 us -> 5.61 us
    ppermute x32 -> x0, starting transfers between devices: 119 us -> none  [the longest x16 98.8 us: padded_2(): before = lax.ppermute(last, axis, up)]
    pallas_call x0 -> x1, Pallas kernels: none -> 78.4 us  [shards(): pl.pallas_call(functools.partial(kernel, lon_count, lat_count, limit), ou...]
    all_to_all x8 -> x0, starting transfers between devices: 44 us -> none  [the longest x1 10.1 us: shards(): lax.all_to_all(lax.all_to_all(collected, 'lon', split_axis=0, concat_axis...]
    ppermute x32 -> x0, waiting for transfers between devices: 39.9 us -> none  [the longest x16 35.8 us: padded_2(): after = lax.ppermute(first, axis, down)]
    all_to_all x8 -> x0, waiting for transfers between devices: 14.6 us -> none  [the longest x1 5.64 us: shards(): lax.all_to_all(lax.all_to_all(packet, 'lon', split_axis=1, concat_axis=1,...]
    scatter-add x1 -> x0, other arithmetic: 13.8 us -> none  [shards(): forcing = jnp.zeros((ITERS * cells,), jnp.float32).at[landing].add(amounts)]
    unnamed x60 -> x18, local copies, waits for them, and re-layouts: 15.2 us -> 3.5 us
    gather x5 -> x0, local copies, waits for them, and re-layouts: 11.6 us -> none  [the longest x4 10.8 us: shards(): tile_blocks(height)[held_index] * held_feet]
  transfers between devices with their start and end apart: 40 -> 0, of which waited for: 15 -> 0; matrix products, arithmetic and copies ran while one was open for 28% -> 0% of each run, Pallas kernels for 0% -> 0%
where the time goes in v1:
time: 93.4 us; the launch traced here: 93.1 us
  Pallas kernels  78.4 us (84%)
  matrix products  5.61 us (6%)
  local copies, waits for them, and re-layouts  5.23 us (6%)
  other arithmetic  3 us (3%)
    pallas_call x1, Pallas kernels, shards(): pl.pallas_call(functools.partial(kernel, lon_count, lat_count, limit), ou...  78.4 us
    dot_general x4, matrix products, exact_dot(): jnp.dot(left, right, precision=lax.Precision.HIGHEST, preferred_element_t...  4.1 us
    unnamed x18, local copies, waits for them, and re-layouts  3.5 us

profile of v1, /device:TPU:0, one launch (start us, length us, event | category | flops | bytes accessed | tf_op | source)
XLA Modules:
  0.0 93.1 jit_solution(2528267208133572880)
XLA Ops:
  0.6 0.0 copy-start
  0.7 0.8 fusion.20
  1.5 1.3 %fusion.8 = f32[1024]{0:T(1024)S(1)} fusion(s32[1024]{0:T(1024)} %bitcast.18), kind=kOutput, calls=%fused_computation.9 | convolution fusion | flops 68353024 | bytes 8192 | tf_op jit(solution)/shard_map/dot_general | solution.py:338
  2.8 0.0 copy-start.3
  2.8 1.3 %compare_select_fusion.2 = (f32[1024,128]{1,0:T(8,128)S(1)}, f32[1024,128]{1,0:T(8,128)S(1)}, f32[1024,128]{1,0:T(8,128)S(1)}) fusion(f32[1024]{0:T(1024)} %param.17, f32[128]{0:T(128)S(1)} %fusion.28, f32[1024]{0:T(1024)S(1)} %fusion.8, f32[1024]{0:T(1024)S(1)} %get-tuple-element.16, f32[1024]{0:T(1024)S(1)} %get-tuple-element.15), kind=kLoop, calls=%fused_computation.14 | loop fusion | flops 524288 | bytes 1589760 | tf_op jit(solution)/shard_map/mul | solution.py:381
  4.1 0.7 fusion.1
  4.8 0.1 mul.97
  4.9 0.1 mul.98
  5.0 0.2 fusion.9
  5.3 0.1 select_reduce_fusion
  5.4 0.1 mul.93
  5.5 0.1 copy.18
  5.6 0.1 copy.19
  5.7 0.1 pad.1.clone
  5.8 0.7 pad_maximum_fusion.packet_ref
  6.5 2.4 %fusion.11.feet_ref = f32[512,1024]{1,0:T(8,128)} fusion(f32[256,1024]{1,0:T(8,128)S(1)} %copy-done, s32[256]{0:T(256)S(1)} %convert_add_fusion), kind=kOutput, calls=%fused_computation.18 | convolution fusion | flops 1610743808 | bytes 3146752 | tf_op jit(solution)/shard_map/dot_general | solution.py:343
  9.0 78.4 %shard_map.138 = (f32[256,512]{1,0:T(8,128)}, f32[256,512]{1,0:T(8,128)}, f32[256,512]{1,0:T(8,128)}, f32[32,8,128]{2,1,0:T(8,128)}) custom-call(f32[256,512]{1,0:T(8,128)} %eta_ref.1, f32[256,512]{1,0:T(8,128)} %east_ref.1, f32[256,512]{1,0:T(8,128)} %north_ref.1, f32[256,512]{1,0:T(8,128)} %depth_ref.1, f32[32,8,128]{2,1,0:T(8,128)} %pad_maximum_fusion.packet_ref, ...), custom_call_target="tpu_custom_call" | custom-call | tf_op jit(solution)/shard_map/pallas_call | solution.py:406
  87.4 1.1 %dynamic-slice_bitcast_fusion = f32[4,32,16]{2,0,1:T(4,128)S(1)} fusion(f32[32,8,128]{2,1,0:T(8,128)} %get-tuple-element.11, s32[]{:T(128)S(6)} %select_n.32), kind=kLoop, calls=%fused_computation.27 | loop fusion | bytes 16388 | tf_op jit(solution)/shard_map/transpose | solution.py:437
  88.5 0.1 reshape.53
  88.6 0.3 fusion.10
  88.9 0.7 fusion.30
  89.6 1.9 %copy.24 = f32[256,512]{1,0:T(8,128)} copy(f32[256,512]{1,0:T(8,128)} %get-tuple-element.21) | data formatting | bytes 1048576
  91.5 0.8 copy.25
  92.3 0.8 copy.26
  (21 shorter events, 0.1 us)
Async XLA Ops:
  0.6 5.9 %copy-start = (f32[256,1024]{1,0:T(8,128)S(1)}, f32[256,1024]{1,0:T(8,128)}, u32[]{:S(2)}) copy-start(f32[256,1024]{1,0:T(8,128)} %param.18) | copy-start | bytes 3145732
  0.6 3.5 %copy-start.5 = (s32[1024,1]{0,1:T(1,128)S(1)}, s32[1024,1]{0,1:T(1,128)}, u32[]{:S(2)}) copy-start(s32[1024,1]{0,1:T(1,128)} %param.15) | copy-start | bytes 12292
  2.8 2.2 %copy-start.3 = (s32[256,1]{0,1:T(1,128)S(1)}, s32[256,1]{0,1:T(1,128)}, u32[]{:S(2)}) copy-start(s32[256,1]{0,1:T(1,128)} %param.19) | copy-start | bytes 3076
  2.8 2.4 %copy-start.4 = (s32[256]{0:T(256)S(1)}, s32[256]{0:T(256)}, u32[]{:S(2)}) copy-start(s32[256]{0:T(256)} %param.20) | copy-start | bytes 3076
  9.0 79.7 %copy-start.6 = (s32[256]{0:T(256)S(1)}, s32[256]{0:T(256)}, u32[]{:S(2)}) copy-start(s32[256]{0:T(256)} %param.21) | copy-start | bytes 3076
  87.4 4.1 %copy-start.2 = (f32[256,512]{1,0:T(8,128)S(1)}, f32[256,512]{1,0:T(8,128)}, u32[]{:S(2)}) copy-start(f32[256,512]{1,0:T(8,128)} %get-tuple-element.22) | copy-start | bytes 1572868
  87.4 4.9 %copy-start.1 = (f32[256,512]{1,0:T(8,128)S(1)}, f32[256,512]{1,0:T(8,128)}, u32[]{:S(2)}) copy-start(f32[256,512]{1,0:T(8,128)} %get-tuple-element.23) | copy-start | bytes 1572868

commit v2 on v1

--- a/solution.py
+++ b/solution.py
@@ -66,6 +66,7 @@
     from_east,
     blocks,
     partial,
+    ids_ref,
     sta_send,
     sta_recv,
     foot_send,
@@ -90,6 +91,13 @@
     def peer(i):
         return lax.rem(me + i, devices)
 
+    def spread_peer(i):
+        turn = lax.rem(i, lat_count)
+        turn = lax.rem(turn, 2) * (lat_count // 2) + turn // 2
+        return lax.rem(lon + i // lat_count, lon_count) * lat_count + lax.rem(
+            lat + turn, lat_count
+        )
+
     def place(d):
         return (d // lat_count, lax.rem(d, lat_count))
 
@@ -134,13 +142,13 @@
     def start_feet(low, high):
         @pl.loop(low, high)
         def _(i):
-            foot_copy(peer(i), me).start()
+            foot_copy(spread_peer(i), me).start()
 
     @pl.loop(1, devices)
     def _(i):
         sta_copy(peer(i), me).start()
 
-    first = 1 + devices // 4
+    first = 1 + 3 * devices // 8
     second = first + devices // 8
     start_feet(1, first)
 
@@ -300,28 +308,37 @@
     number = lax.broadcasted_iota(jnp.int32, (count, LANES), 0)
     number = (lax.rem(number, bands) * block_cols + number // bands).astype(F32)
 
-    @pl.loop(1, devices)
-    def _(i):
-        foot_copy(me, peer(i)).wait_recv()
-
     for g in range(group):
-        foot_high, foot_low = split(held[g * LANES : (g + 1) * LANES, :])
+        ids_ref[g] = jnp.broadcast_to(ids[g : g + 1, :], (8, LANES))
+        partial[g] = jnp.zeros((8, LANES), F32)
+    mine = me // per_group
+
+    @pl.loop(0, group)
+    def _(j):
+        g = lax.rem(mine + group - j, group)
+
+        @pl.loop(0, per_group)
+        def _(t):
+            source = g * per_group + t
+            pl.when(source != me)(foot_copy(me, source).wait_recv)
+
+        foot_high, foot_low = split(held[pl.ds(pl.multiple_of(g * LANES, LANES), LANES), :])
         both = (
             nt_dot(block_high, foot_high)
             + nt_dot(block_high, foot_low)
             + nt_dot(block_low, foot_high)
         )
-        wanted = number == ids[g : g + 1, :]
+        wanted = number == ids_ref[g][:1]
         for k in range(ITERS):
             found = jnp.where(wanted, both[k * count : (k + 1) * count], 0.0)
             partial[g, k : k + 1, :] = jnp.sum(found, axis=0, keepdims=True)
-        partial[g, ITERS:, :] = jnp.zeros((8 - ITERS, LANES), F32)
-
-    @pl.loop(1, devices)
-    def _(i):
-        back_copy(peer(i), me).start()
-
-    back_out[me] = partial[me // per_group]
+
+        @pl.loop(0, per_group)
+        def _(t):
+            owner = g * per_group + t
+            pl.when(owner != me)(back_copy(owner, me).start)
+
+    back_out[me] = partial[mine]
 
     @pl.loop(1, devices)
     def _(i):
@@ -418,6 +435,7 @@
             pltpu.VMEM((rows, LANES), F32),
             pltpu.VMEM((ITERS * count, BH * BW), F32),
             pltpu.VMEM((group, 8, LANES), F32),
+            pltpu.VMEM((group, 8, LANES), F32),
             pltpu.SemaphoreType.DMA((devices,)),
             pltpu.SemaphoreType.DMA((devices,)),
             pltpu.SemaphoreType.DMA((devices,)),

time: 93.4 us -> 86.6 us (0.927)
  Pallas kernels: 78.4 us -> 71.6 us
    pallas_call x1, Pallas kernels: 78.4 us -> 71.6 us  [shards(): pl.pallas_call(functools.partial(kernel, lon_count, lat_count, limit), ou...]
where the time goes in v2:
time: 86.6 us; the launch traced here: 86.3 us
  Pallas kernels  71.6 us (83%)
  matrix products  5.61 us (6%)
  local copies, waits for them, and re-layouts  5.23 us (6%)
  other arithmetic  3 us (3%)
    pallas_call x1, Pallas kernels, shards(): pl.pallas_call(functools.partial(kernel, lon_count, lat_count, limit), ou...  71.6 us
    dot_general x4, matrix products, exact_dot(): jnp.dot(left, right, precision=lax.Precision.HIGHEST, preferred_element_t...  4.1 us
    unnamed x18, local copies, waits for them, and re-layouts  3.5 us

profile of v2, /device:TPU:0, one launch (start us, length us, event | category | flops | bytes accessed | tf_op | source)
XLA Modules:
  0.0 86.3 jit_solution(3764164666888603448)
XLA Ops:
  0.6 0.0 copy-start
  0.6 0.0 copy-start.5
  0.7 0.8 fusion.20
  1.5 1.3 %fusion.8 = f32[1024]{0:T(1024)S(1)} fusion(s32[1024]{0:T(1024)} %bitcast.18), kind=kOutput, calls=%fused_computation.9 | convolution fusion | flops 68353024 | bytes 8192 | tf_op jit(solution)/shard_map/dot_general | solution.py:355
  2.8 1.3 %compare_select_fusion.2 = (f32[1024,128]{1,0:T(8,128)S(1)}, f32[1024,128]{1,0:T(8,128)S(1)}, f32[1024,128]{1,0:T(8,128)S(1)}) fusion(f32[1024]{0:T(1024)} %param.17, f32[128]{0:T(128)S(1)} %fusion.28, f32[1024]{0:T(1024)S(1)} %fusion.8, f32[1024]{0:T(1024)S(1)} %get-tuple-element.16, f32[1024]{0:T(1024)S(1)} %get-tuple-element.15), kind=kLoop, calls=%fused_computation.14 | loop fusion | flops 524288 | bytes 1589760 | tf_op jit(solution)/shard_map/mul | solution.py:398
  4.1 0.7 fusion.1
  4.8 0.1 mul.97
  4.9 0.1 mul.98
  5.0 0.2 fusion.9
  5.3 0.1 select_reduce_fusion
  5.4 0.1 mul.93
  5.5 0.1 copy.18
  5.6 0.1 copy.19
  5.7 0.1 pad.1.clone
  5.8 0.7 pad_maximum_fusion.packet_ref
  6.5 2.4 %fusion.11.feet_ref = f32[512,1024]{1,0:T(8,128)} fusion(f32[256,1024]{1,0:T(8,128)S(1)} %copy-done, s32[256]{0:T(256)S(1)} %convert_add_fusion), kind=kOutput, calls=%fused_computation.18 | convolution fusion | flops 1610743808 | bytes 3146752 | tf_op jit(solution)/shard_map/dot_general | solution.py:360
  9.0 71.6 %shard_map.138 = (f32[256,512]{1,0:T(8,128)}, f32[256,512]{1,0:T(8,128)}, f32[256,512]{1,0:T(8,128)}, f32[32,8,128]{2,1,0:T(8,128)}) custom-call(f32[256,512]{1,0:T(8,128)} %eta_ref.1, f32[256,512]{1,0:T(8,128)} %east_ref.1, f32[256,512]{1,0:T(8,128)} %north_ref.1, f32[256,512]{1,0:T(8,128)} %depth_ref.1, f32[32,8,128]{2,1,0:T(8,128)} %pad_maximum_fusion.packet_ref, ...), custom_call_target="tpu_custom_call" | custom-call | tf_op jit(solution)/shard_map/pallas_call | solution.py:423
  80.6 1.1 %dynamic-slice_bitcast_fusion = f32[4,32,16]{2,0,1:T(4,128)S(1)} fusion(f32[32,8,128]{2,1,0:T(8,128)} %get-tuple-element.11, s32[]{:T(128)S(6)} %select_n.32), kind=kLoop, calls=%fused_computation.27 | loop fusion | bytes 16388 | tf_op jit(solution)/shard_map/transpose | solution.py:455
  81.7 0.1 reshape.53
  81.8 0.3 fusion.10
  82.1 0.7 fusion.30
  82.8 1.9 %copy.24 = f32[256,512]{1,0:T(8,128)} copy(f32[256,512]{1,0:T(8,128)} %get-tuple-element.21) | data formatting | bytes 1048576
  84.7 0.8 copy.25
  85.5 0.8 copy.26
  (21 shorter events, 0.1 us)
Async XLA Ops:
  0.6 5.9 %copy-start = (f32[256,1024]{1,0:T(8,128)S(1)}, f32[256,1024]{1,0:T(8,128)}, u32[]{:S(2)}) copy-start(f32[256,1024]{1,0:T(8,128)} %param.18) | copy-start | bytes 3145732
  0.6 3.5 %copy-start.5 = (s32[1024,1]{0,1:T(1,128)S(1)}, s32[1024,1]{0,1:T(1,128)}, u32[]{:S(2)}) copy-start(s32[1024,1]{0,1:T(1,128)} %param.15) | copy-start | bytes 12292
  2.8 2.2 %copy-start.3 = (s32[256,1]{0,1:T(1,128)S(1)}, s32[256,1]{0,1:T(1,128)}, u32[]{:S(2)}) copy-start(s32[256,1]{0,1:T(1,128)} %param.19) | copy-start | bytes 3076
  2.8 2.4 %copy-start.4 = (s32[256]{0:T(256)S(1)}, s32[256]{0:T(256)}, u32[]{:S(2)}) copy-start(s32[256]{0:T(256)} %param.20) | copy-start | bytes 3076
  9.0 72.9 %copy-start.6 = (s32[256]{0:T(256)S(1)}, s32[256]{0:T(256)}, u32[]{:S(2)}) copy-start(s32[256]{0:T(256)} %param.21) | copy-start | bytes 3076
  80.6 4.1 %copy-start.2 = (f32[256,512]{1,0:T(8,128)S(1)}, f32[256,512]{1,0:T(8,128)}, u32[]{:S(2)}) copy-start(f32[256,512]{1,0:T(8,128)} %get-tuple-element.22) | copy-start | bytes 1572868
  80.6 4.9 %copy-start.1 = (f32[256,512]{1,0:T(8,128)S(1)}, f32[256,512]{1,0:T(8,128)}, u32[]{:S(2)}) copy-start(f32[256,512]{1,0:T(8,128)} %get-tuple-element.23) | copy-start | bytes 1572868
